TPU v7x, 512 devices: a whole 4x8x8 slice. The times are simulated.
512 devices in a mesh: pool: 32 (over z, x), tp: 16 (over y, core).
Axes of the slice: x: 4, y: 8, z: 8, core: 2. Of those that a mesh axis runs over, the one named last changes fastest.
Arguments:
- activations: bfloat16 [2, 256, 8192], P(None, None, 'tp'), may hold values from -6 to 6
- gate_matrix: bfloat16 [8192, 28672], P('tp', 'pool'), may hold values from -0.0625 to 0.0625
- up_weight: bfloat16 [8192, 28672], P('tp', 'pool'), may hold values from -0.0625 to 0.0625
- down_matrix: bfloat16 [28672, 8192], P('pool', 'tp'), may hold values from -0.03125 to 0.03125
- shrink_pages: bfloat16 [128, 64, 8192], P('pool', None, 'tp'), may hold values from -0.0625 to 0.0625
- expand_pages: bfloat16 [128, 64, 28672], P('pool', 'tp'), may hold values from -0.75 to 0.75
- row_adapter: int32 [2, 256], replicated, may hold values from 0 to 127, as said below
- page_table: int32 [128], replicated, may hold values from 0 to 127, as said below
Outputs:
- layer_out: bfloat16 [2, 256, 8192], P(None, None, 'tp')
Inputs may be any that keep to these rules, and one draw needn't show every extreme that they name: `row_adapter`: in each micro-batch, the rows use at most 1 distinct adapter among those whose pages have the same owner, the owner of page g being g // 4 (so a micro-batch may use up to 32 adapters, one per owner). A permutation: adapter a is stored at page page_table[a].
All inputs are finite; a program needn't handle non-finite values.
Results may differ from a plain program's by a relative error of at most 0.0057.
Values may be sent and summed in bfloat16 or wider, within the bound.
A program may use at most 64 MiB of HBM per device.

v0:
```python
import functools
import jax
import jax.numpy as jnp
from jax import lax
from jax.sharding import Mesh
from jax.sharding import PartitionSpec as P

CAP = 1
POOL = ("pool_0", "pool_1")
adapter_scale = 2.0


def in_blocks(value, dim, size):
    before, after = (value.shape[:dim], value.shape[dim + 1 :])
    return jnp.moveaxis(value.reshape(*before, size, -1, *after), dim, 0)


def sum_at_owner(value, axis, dim):
    size = lax.axis_size(axis)
    pieces = lax.all_to_all(in_blocks(value, dim, size), axis, 0, 0, tiled=True)
    return jnp.sum(pieces, axis=0)


def copy_for_each(value, axis):
    copies = jnp.broadcast_to(value, (lax.axis_size(axis), *value.shape))
    return lax.all_to_all(copies, axis, split_axis=0, concat_axis=0, tiled=True)


def over_copies(value, axis):
    everything = copy_for_each(value, axis)
    return jnp.sum(everything, axis=0)


def by_axis(value, axes):
    return functools.reduce(lax.psum, axes, value)


def on_device(
    activations,
    gate_matrix,
    up_weight,
    down_matrix,
    shrink_pages,
    expand_pages,
    row_adapter,
    page_table,
):
    pool_count = lax.axis_size(POOL)
    pool_index = lax.axis_index(POOL)
    batches, row_count, local_width = activations.shape
    page_count = shrink_pages.shape[0]
    rank_local = expand_pages.shape[1]
    hidden_local = gate_matrix.shape[1]
    adapter_total = page_table.shape[0]
    catalog = jnp.arange(adapter_total, dtype=jnp.int32)
    page_of_row = jnp.sum(jnp.where(row_adapter[:, :, None] == catalog, page_table, 0), axis=2)
    groups = [(batch_index, batch_index + 1) for batch_index in range(batches)]
    outputs = []
    for group_start, group_stop in groups:
        group_size = group_stop - group_start
        rows_in = activations[group_start:group_stop].reshape(group_size * row_count, local_width)
        pages_in = page_of_row[group_start:group_stop]
        row_pages = pages_in.reshape(-1)
        row_owner = row_pages // page_count
        row_local = row_pages % page_count
        row_total = group_size * row_count
        projected = jnp.einsum(
            "nd,prd->npr", rows_in, shrink_pages, preferred_element_type=jnp.float32
        )
        owned_here = (row_owner == pool_index)[:, None] & (
            row_local[:, None] == jnp.arange(page_count, dtype=jnp.int32)
        )
        shrink_part = jnp.sum(jnp.where(owned_here[:, :, None], projected, 0.0), axis=1)
        rank_share = sum_at_owner(shrink_part, "tp", 1)
        shrink_mine = over_copies(rank_share, POOL).astype(jnp.bfloat16)
        page_used = jnp.any(pages_in[:, :, None] == catalog, axis=1)
        page_order = jnp.cumsum(page_used.astype(jnp.int32), axis=1) - 1
        owner_order = (
            page_order.reshape(group_size, pool_count, page_count)
            - lax.dynamic_index_in_dim(page_order.reshape(group_size, pool_count, page_count), 0, 2)
            + page_used.reshape(group_size, pool_count, page_count)[:, :, :1].astype(jnp.int32)
            - 1
        )
        owned_used = lax.dynamic_index_in_dim(
            page_used.reshape(group_size, pool_count, page_count), pool_index, 1, keepdims=False
        )
        owned_order = lax.dynamic_index_in_dim(owner_order, pool_index, 1, keepdims=False)
        hit_table = owned_used[:, :, None] & (
            owned_order[:, :, None] == jnp.arange(CAP, dtype=jnp.int32)
        )
        chosen = jnp.sum(
            jnp.where(hit_table, jnp.arange(page_count, dtype=jnp.int32)[None, :, None], 0), axis=1
        )
        outgoing = jnp.take(expand_pages, chosen.reshape(-1), axis=0)
        outgoing = outgoing.reshape(group_size * CAP, rank_local, pool_count, hidden_local)
        received = lax.all_to_all(outgoing, POOL, split_axis=2, concat_axis=0, tiled=True)
        blocks_mat = received.reshape(pool_count * group_size * CAP * rank_local, hidden_local)
        slot_total = pool_count * group_size * CAP
        flat_order = owner_order.reshape(group_size, adapter_total)
        row_order = jnp.sum(
            jnp.where(pages_in[:, :, None] == catalog, flat_order[:, None, :], 0), axis=2
        )
        batch_of_row = lax.broadcasted_iota(jnp.int32, (group_size, row_count), 0)
        slot_of_row = (
            (pages_in // page_count * group_size + batch_of_row) * CAP + row_order
        ).reshape(-1)
        onehot = slot_of_row[:, None] == jnp.arange(slot_total, dtype=jnp.int32)
        wide_rows = jnp.where(
            onehot[:, :, None], shrink_mine[:, None, :], jnp.zeros((), jnp.bfloat16)
        )
        wide_rows = wide_rows.reshape(row_total, slot_total * rank_local)
        gate_term = jnp.dot(rows_in, gate_matrix, preferred_element_type=jnp.float32)
        up_product = jnp.dot(rows_in, up_weight, preferred_element_type=jnp.float32)
        up_product = up_product + adapter_scale * jnp.dot(
            wide_rows, blocks_mat, preferred_element_type=jnp.float32
        )
        summed = lax.psum_scatter(
            jnp.concatenate([gate_term, up_product], axis=1), "tp", scatter_dimension=0, tiled=True
        )
        hidden = (jax.nn.silu(summed[:, :hidden_local]) * summed[:, hidden_local:]).astype(
            jnp.bfloat16
        )
        partial_out = jnp.dot(
            lax.all_gather(hidden, "tp", axis=0, tiled=True),
            down_matrix,
            preferred_element_type=jnp.float32,
        )
        out_total = by_axis(partial_out, POOL)
        outputs.append(out_total.astype(jnp.bfloat16).reshape(group_size, row_count, local_width))
    return jnp.concatenate(outputs, axis=0)


def solution(mesh):
    split = Mesh(mesh.devices.reshape(8, 4, mesh.shape["tp"]), ("pool_0", "pool_1", "tp"))
    return jax.shard_map(
        on_device,
        mesh=split,
        in_specs=(
            P(None, None, "tp"),
            P("tp", POOL),
            P("tp", POOL),
            P(POOL, "tp"),
            P(POOL, None, "tp"),
            P(POOL, "tp", None),
            P(),
            P(),
        ),
        out_specs=P(None, None, "tp"),
        check_vma=False,
    )
```

profile of v0, /device:TPU:8, one launch (start us, length us, event | category | flops | bytes accessed | tf_op | source)
XLA Modules:
  0.0 339.3 jit_solution(7243623281947806800)
XLA Ops:
  6.5 1.1 select_reduce_fusion
  7.7 1.3 fusion.2
  9.6 9.1 %all-to-all-start = ((f32[16,256,4]{1,2,0:T(4,128)}), f32[16,256,4]{1,2,0:T(4,128)S(1)}, u32[]{:S(2)}, u32[]{:S(2)}) async-start(f32[16,256,4]{1,2,0:T(4,128)} %bitcast.7), calls=%async_computation | async-start | bytes 131072 | tf_op jit(solution)/shard_map/all_to_all | solution.py:20
  23.0 3.2 fusion.38
  31.3 2.3 fusion.10
  33.6 1.0 dynamic-slice_select_fusion.1
  35.3 11.7 %all-to-all-start.1 = ((f32[32,256,4]{1,2,0:T(4,128)}), f32[32,256,4]{1,2,0:T(4,128)S(1)}, u32[]{:S(2)}, u32[]{:S(2)}) async-start(f32[32,256,4]{1,2,0:T(4,128)} %broadcast_in_dim.130), calls=%async_computation.1 | async-start | bytes 262144 | tf_op jit(solution)/shard_map/all_to_all | solution.py:26
  47.4 10.3 %all-to-all-done.1 = f32[32,256,4]{1,2,0:T(4,128)S(1)} async-done(((f32[32,256,4]{1,2,0:T(4,128)}), f32[32,256,4]{1,2,0:T(4,128)S(1)}, u32[]{:S(2)}, u32[]{:S(2)}) %all-to-all-start.1) | async-done | bytes 131104 | tf_op jit(solution)/shard_map/all_to_all | solution.py:26
  58.4 3.9 %all-to-all-start.2 = ((bf16[1,4,32,896]{3,1,0,2:T(4,128)(2,1)}), bf16[1,4,32,896]{3,1,0,2:T(4,128)(2,1)S(1)}, u32[]{:S(2)}, u32[]{:S(2)}) async-start(bf16[1,4,32,896]{3,1,0,2:T(4,128)(2,1)} %bitcast.12), calls=%async_computation.2 | async-start | bytes 458752 | tf_op jit(solution)/shard_map/all_to_all | solution.py:96
  62.3 1.0 reduce_sum.108
  64.0 1.5 select_n.160
  65.5 8.2 %all-to-all-done.2 = bf16[1,4,32,896]{3,1,0,2:T(4,128)(2,1)S(1)} async-done(((bf16[1,4,32,896]{3,1,0,2:T(4,128)(2,1)}), bf16[1,4,32,896]{3,1,0,2:T(4,128)(2,1)S(1)}, u32[]{:S(2)}, u32[]{:S(2)}) %all-to-all-start.2) | async-done | bytes 229408 | tf_op jit(solution)/shard_map/all_to_all | solution.py:96
  74.4 1.0 reshape.821
  75.4 1.5 fusion.1
  76.9 1.4 pad_maximum_fusion
  80.1 7.2 %all-to-all-start.3 = ((f32[16,256,4]{1,2,0:T(4,128)}), f32[16,256,4]{1,2,0:T(4,128)S(1)}, u32[]{:S(2)}, u32[]{:S(2)}) async-start(f32[16,256,4]{1,2,0:T(4,128)} %bitcast.23), calls=%async_computation.4 | async-start | bytes 131072 | tf_op jit(solution)/shard_map/all_to_all | solution.py:20
  87.4 1.4 fusion.5
  88.7 5.2 %all-to-all-done.3 = f32[16,256,4]{1,2,0:T(4,128)S(1)} async-done(((f32[16,256,4]{1,2,0:T(4,128)}), f32[16,256,4]{1,2,0:T(4,128)S(1)}, u32[]{:S(2)}, u32[]{:S(2)}) %all-to-all-start.3) | async-done | bytes 65568 | tf_op jit(solution)/shard_map/all_to_all | solution.py:20
  94.6 3.9 %all-to-all-start.4 = ((f32[32,256,4]{1,2,0:T(4,128)}), f32[32,256,4]{1,2,0:T(4,128)S(1)}, u32[]{:S(2)}, u32[]{:S(2)}) async-start(f32[32,256,4]{1,2,0:T(4,128)} %broadcast_in_dim.136), calls=%async_computation.5 | async-start | bytes 262144 | tf_op jit(solution)/shard_map/all_to_all | solution.py:26
  98.9 10.7 %all-to-all-done.4 = f32[32,256,4]{1,2,0:T(4,128)S(1)} async-done(((f32[32,256,4]{1,2,0:T(4,128)}), f32[32,256,4]{1,2,0:T(4,128)S(1)}, u32[]{:S(2)}, u32[]{:S(2)}) %all-to-all-start.4) | async-done | bytes 131104 | tf_op jit(solution)/shard_map/all_to_all | solution.py:26
  109.7 3.9 %all-to-all-start.5 = ((bf16[1,4,32,896]{3,1,0,2:T(4,128)(2,1)}), bf16[1,4,32,896]{3,1,0,2:T(4,128)(2,1)S(1)}, u32[]{:S(2)}, u32[]{:S(2)}) async-start(bf16[1,4,32,896]{3,1,0,2:T(4,128)(2,1)} %bitcast.28), calls=%async_computation.6 | async-start | bytes 458752 | tf_op jit(solution)/shard_map/all_to_all | solution.py:96
  113.7 11.6 %all-to-all-done.5 = bf16[1,4,32,896]{3,1,0,2:T(4,128)(2,1)S(1)} async-done(((bf16[1,4,32,896]{3,1,0,2:T(4,128)(2,1)}), bf16[1,4,32,896]{3,1,0,2:T(4,128)(2,1)S(1)}, u32[]{:S(2)}, u32[]{:S(2)}) %all-to-all-start.5) | async-done | bytes 229408 | tf_op jit(solution)/shard_map/all_to_all | solution.py:96
  125.4 1.5 fusion
  126.9 1.3 pad_maximum_fusion.1
  128.3 4.0 %reduce-scatter.3.cloned.1.call-done = f32[16,1792]{1,0:T(8,128)} async-done(((f32[256,1792]{1,0:T(8,128)}), f32[16,1792]{1,0:T(8,128)}) %reduce-scatter.3.cloned.1.call-update) | async-done | bytes 114704 | tf_op jit(solution)/shard_map/reduce_scatter | solution.py:117
  133.1 18.9 %all_gather.6 = bf16[256,896]{1,0:T(8,128)(2,1)S(1)} all-gather(bf16[16,896]{1,0:T(8,128)(2,1)S(1)} %fusion.23), channel_id=1, replica_groups=mesh['pool_0'=8,'pool_1'=4,'tp'=16] {'tp'}, dimensions={0}, use_global_device_ids=true | all-gather | bytes 487424 | tf_op jit(solution)/shard_map/all_gather | solution.py:124
  152.0 43.8 %reduce-scatter.5.cloned.1.call-done = f32[16,1792]{1,0:T(8,128)} async-done(((f32[256,1792]{1,0:T(8,128)}), f32[16,1792]{1,0:T(8,128)}) %reduce-scatter.5.cloned.1.call-update) | async-done | bytes 114704 | tf_op jit(solution)/shard_map/reduce_scatter | solution.py:117
  196.7 18.9 %all_gather.7 = bf16[256,896]{1,0:T(8,128)(2,1)S(1)} all-gather(bf16[16,896]{1,0:T(8,128)(2,1)S(1)} %fusion.22), channel_id=1, replica_groups=mesh['pool_0'=8,'pool_1'=4,'tp'=16] {'tp'}, dimensions={0}, use_global_device_ids=true | all-gather | bytes 487424 | tf_op jit(solution)/shard_map/all_gather | solution.py:124
  215.6 1.3 fusion.41
  216.8 1.2 fusion.42
  218.1 81.7 %all-reduce.5.cloned.1.call-done = (f32[256,512]{1,0:T(8,128)}, f32[256,512]{1,0:T(8,128)}) async-done(((f32[256,512]{1,0:T(8,128)}, f32[256,512]{1,0:T(8,128)}), (f32[256,512]{1,0:T(8,128)}, f32[256,512]{1,0:T(8,128)})) %all-reduce.5.cloned.1.call-update) | async-done | bytes 1048592 | tf_op jit(solution)/shard_map/psum | solution.py:35
  299.8 32.1 %all-reduce.6 = (bf16[256,512]{1,0:T(8,128)(2,1)S(1)}, bf16[256,512]{1,0:T(8,128)(2,1)S(1)}) all-reduce(f32[256,512]{1,0:T(8,128)} %get-tuple-element.17, f32[256,512]{1,0:T(8,128)} %get-tuple-element.18), channel_id=1, replica_groups=mesh['pool_0'=8,'pool_1'=4,'tp'=16] {'pool_1'}, use_global_device_ids=true, to_apply=%region_20.22 | all-reduce | flops 262144 | bytes 1572864 | tf_op jit(solution)/shard_map/psum | solution.py:35
  (80 shorter events, 15.2 us)
Async XLA Ops:
  6.5 24.7 %copy-start = (bf16[512,896]{1,0:T(8,128)(2,1)S(1)}, bf16[512,896]{1,0:T(8,128)(2,1)}, u32[]{:S(2)}) copy-start(bf16[512,896]{1,0:T(8,128)(2,1)} %param.12) | copy-start | bytes 2752516
  6.5 27.1 %copy-start.6 = (bf16[4,4,28672]{2,1,0:T(4,128)(2,1)S(1)}, bf16[4,4,28672]{2,1,0:T(4,128)(2,1)}, u32[]{:S(2)}) copy-start(bf16[4,4,28672]{2,1,0:T(4,128)(2,1)} %param.15) | copy-start | bytes 2752516
  9.6 25.0 %all-to-all-start = ((f32[16,256,4]{1,2,0:T(4,128)}), f32[16,256,4]{1,2,0:T(4,128)S(1)}, u32[]{:S(2)}, u32[]{:S(2)}) async-start(f32[16,256,4]{1,2,0:T(4,128)} %bitcast.7), calls=%async_computation | async-start | bytes 131072 | tf_op jit(solution)/shard_map/all_to_all | solution.py:20
  27.4 19.6 %copy-start.1 = (bf16[512,896]{1,0:T(8,128)(2,1)S(1)}, bf16[512,896]{1,0:T(8,128)(2,1)}, u32[]{:S(2)}) copy-start(bf16[512,896]{1,0:T(8,128)(2,1)} %param.11) | copy-start | bytes 2752516
  27.4 19.6 %copy-start.3 = (bf16[2,256,512]{2,1,0:T(8,128)(2,1)S(1)}, bf16[2,256,512]{2,1,0:T(8,128)(2,1)}, u32[]{:S(2)}) copy-start(bf16[2,256,512]{2,1,0:T(8,128)(2,1)} %param.10) | copy-start | bytes 1572868
  35.3 22.4 %all-to-all-start.1 = ((f32[32,256,4]{1,2,0:T(4,128)}), f32[32,256,4]{1,2,0:T(4,128)S(1)}, u32[]{:S(2)}, u32[]{:S(2)}) async-start(f32[32,256,4]{1,2,0:T(4,128)} %broadcast_in_dim.130), calls=%async_computation.1 | async-start | bytes 262144 | tf_op jit(solution)/shard_map/all_to_all | solution.py:26
  57.7 0.7 copy-start.5
  58.4 15.3 %all-to-all-start.2 = ((bf16[1,4,32,896]{3,1,0,2:T(4,128)(2,1)}), bf16[1,4,32,896]{3,1,0,2:T(4,128)(2,1)S(1)}, u32[]{:S(2)}, u32[]{:S(2)}) async-start(bf16[1,4,32,896]{3,1,0,2:T(4,128)(2,1)} %bitcast.12), calls=%async_computation.2 | async-start | bytes 458752 | tf_op jit(solution)/shard_map/all_to_all | solution.py:96
  62.3 70.0 %reduce-scatter.3.cloned.1.call-start = ((), (), s32[]{:S(2)}) async-start(), calls=%async_computation.8 | async-start | bytes 1949696 | tf_op jit(solution)/shard_map/reduce_scatter | solution.py:117
  73.7 0.7 copy-start.4
  78.3 0.9 copy-start.7
  80.1 13.8 %all-to-all-start.3 = ((f32[16,256,4]{1,2,0:T(4,128)}), f32[16,256,4]{1,2,0:T(4,128)S(1)}, u32[]{:S(2)}, u32[]{:S(2)}) async-start(f32[16,256,4]{1,2,0:T(4,128)} %bitcast.23), calls=%async_computation.4 | async-start | bytes 131072 | tf_op jit(solution)/shard_map/all_to_all | solution.py:20
  94.6 15.0 %all-to-all-start.4 = ((f32[32,256,4]{1,2,0:T(4,128)}), f32[32,256,4]{1,2,0:T(4,128)S(1)}, u32[]{:S(2)}, u32[]{:S(2)}) async-start(f32[32,256,4]{1,2,0:T(4,128)} %broadcast_in_dim.136), calls=%async_computation.5 | async-start | bytes 262144 | tf_op jit(solution)/shard_map/all_to_all | solution.py:26
  109.7 15.6 %all-to-all-start.5 = ((bf16[1,4,32,896]{3,1,0,2:T(4,128)(2,1)}), bf16[1,4,32,896]{3,1,0,2:T(4,128)(2,1)S(1)}, u32[]{:S(2)}, u32[]{:S(2)}) async-start(bf16[1,4,32,896]{3,1,0,2:T(4,128)(2,1)} %bitcast.28), calls=%async_computation.6 | async-start | bytes 458752 | tf_op jit(solution)/shard_map/all_to_all | solution.py:96
  113.5 82.3 %reduce-scatter.5.cloned.1.call-start = ((), (), s32[]{:S(2)}) async-start(), calls=%async_computation.9 | async-start | bytes 1949696 | tf_op jit(solution)/shard_map/reduce_scatter | solution.py:117
  128.2 87.4 %copy-start.2 = (bf16[896,512]{1,0:T(8,128)(2,1)S(1)}, bf16[896,512]{1,0:T(8,128)(2,1)}, u32[]{:S(2)}) copy-start(bf16[896,512]{1,0:T(8,128)(2,1)} %param.13) | copy-start | bytes 2752516
  128.2 171.6 %all-reduce.5.cloned.1.call-start = ((), (), s32[]{:S(2)}) async-start(), calls=%async_computation.10 | async-start | bytes 2097152 | tf_op jit(solution)/shard_map/psum | solution.py:35
Sparse Core Ops, SparseCore 0:
  78.4 53.7 reduce-scatter.2
  135.1 60.6 reduce-scatter.4
  218.2 81.5 all-reduce.4
where the time goes:
time: 340 us; the launch traced here: 339 us
  waiting for transfers between devices  175 us (51%)
  blocking collectives  70 us (21%)
  starting transfers between devices  39.7 us (12%)
  between operations  17.3 us (5%)
  other arithmetic  14 us (4%)
  matrix products  11.6 us (3%)
  local copies, waits for them, and re-layouts  11.3 us (3%)
    psum x1, waiting for transfers between devices, by_axis(): return functools.reduce(lax.psum, axes, value)  81.7 us
    reduce_scatter x2, waiting for transfers between devices, on_device(): lax.psum_scatter(jnp.concatenate([gate_term, up_product], axis=1), 'tp',...  47.7 us
    all_gather x2, blocking collectives, on_device(): lax.all_gather(hidden, 'tp', axis=0, tiled=True)  37.8 us
    psum x1, blocking collectives, by_axis(): return functools.reduce(lax.psum, axes, value)  32.1 us
    all_to_all x2, waiting for transfers between devices, copy_for_each(): return lax.all_to_all(copies, axis, split_axis=0, concat_axis=0, tiled=True)  21 us
    all_to_all x2, waiting for transfers between devices, on_device(): lax.all_to_all(outgoing, POOL, split_axis=2, concat_axis=0, tiled=True)  19.8 us
    all_to_all x2, starting transfers between devices, sum_at_owner(): pieces = lax.all_to_all(in_blocks(value, dim, size), axis, 0, 0, tiled=True)  16.3 us
    all_to_all x2, starting transfers between devices, copy_for_each(): return lax.all_to_all(copies, axis, split_axis=0, concat_axis=0, tiled=True)  15.5 us
  transfers between devices with their start and end apart: 9, of which 8 were waited for; matrix products, arithmetic and copies ran while one was open for 7% of the time, Pallas kernels for 0%

commit v1 on v0

--- a/solution.py
+++ b/solution.py
@@ -8,6 +8,27 @@
 CAP = 1
 POOL = ("pool_0", "pool_1")
 adapter_scale = 2.0
+
+
+def ring_gather(x, axis, dim):
+    devices, index, extent = (lax.axis_size(axis), lax.axis_index(axis), x.shape[dim])
+    right = [(i, (i + 1) % devices) for i in range(devices)]
+    downward = [(i, (i - 1) % devices) for i in range(devices)]
+    out = jnp.zeros((*x.shape[:dim], devices * extent, *x.shape[dim + 1 :]), x.dtype)
+    out = lax.dynamic_update_slice_in_dim(out, x, index * extent, axis=dim)
+    from_left = from_right = x
+    middle = devices // 2
+    for step in range(1, middle + 1):
+        from_left = lax.ppermute(from_left, axis, right)
+        out = lax.dynamic_update_slice_in_dim(
+            out, from_left, (index - step) % devices * extent, axis=dim
+        )
+        if step < devices - middle:
+            from_right = lax.ppermute(from_right, axis, downward)
+            out = lax.dynamic_update_slice_in_dim(
+                out, from_right, (index + step) % devices * extent, axis=dim
+            )
+    return out
 
 
 def in_blocks(value, dim, size):
@@ -121,9 +142,7 @@
             jnp.bfloat16
         )
         partial_out = jnp.dot(
-            lax.all_gather(hidden, "tp", axis=0, tiled=True),
-            down_matrix,
-            preferred_element_type=jnp.float32,
+            ring_gather(hidden, "tp", 0), down_matrix, preferred_element_type=jnp.float32
         )
         out_total = by_axis(partial_out, POOL)
         outputs.append(out_total.astype(jnp.bfloat16).reshape(group_size, row_count, local_width))

time: 340 us -> 368 us (1.082)
  starting transfers between devices: 39.7 us -> 78.1 us
  blocking collectives: 70 us -> 32.1 us
  waiting for transfers between devices: 175 us -> 205 us
    all_gather x2 -> x0, blocking collectives: 37.8 us -> none  [on_device(): lax.all_gather(hidden, 'tp', axis=0, tiled=True)]
    ppermute x0 -> x30, starting transfers between devices: none -> 37.7 us  [the longest x14 37.6 us: ring_gather(): from_right = lax.ppermute(from_right, axis, downward)]
    reduce_scatter x2, waiting for transfers between devices: 47.7 us -> 64.9 us  [on_device(): lax.psum_scatter(jnp.concatenate([gate_term, up_product], axis=1), 'tp',...]
    psum x1, waiting for transfers between devices: 81.7 us -> 87 us  [by_axis(): return functools.reduce(lax.psum, axes, value)]
    ppermute x0 -> x30, waiting for transfers between devices: none -> 4.45 us  [the longest x16 4.41 us: ring_gather(): from_left = lax.ppermute(from_left, axis, right)]
  transfers between devices with their start and end apart: 9 -> 39, of which waited for: 8 -> 10; matrix products, arithmetic and copies ran while one was open for 7% -> 7% of each run, Pallas kernels for 0% -> 0%
where the time goes in v1:
time: 368 us; the launch traced here: 367 us
  waiting for transfers between devices  205 us (56%)
  starting transfers between devices  78.1 us (21%)
  blocking collectives  32.1 us (9%)
  between operations  17.8 us (5%)
  other arithmetic  13.5 us (4%)
  matrix products  11.6 us (3%)
  local copies, waits for them, and re-layouts  9.57 us (3%)
    psum x1, waiting for transfers between devices, by_axis(): return functools.reduce(lax.psum, axes, value)  87 us
    reduce_scatter x2, waiting for transfers between devices, on_device(): lax.psum_scatter(jnp.concatenate([gate_term, up_product], axis=1), 'tp',...  64.9 us
    ppermute x14, starting transfers between devices, ring_gather(): from_right = lax.ppermute(from_right, axis, downward)  37.6 us
    psum x1, blocking collectives, by_axis(): return functools.reduce(lax.psum, axes, value)  32.1 us
    all_to_all x2, waiting for transfers between devices, on_device(): lax.all_to_all(outgoing, POOL, split_axis=2, concat_axis=0, tiled=True)  22.1 us
    all_to_all x2, waiting for transfers between devices, copy_for_each(): return lax.all_to_all(copies, axis, split_axis=0, concat_axis=0, tiled=True)  21 us
    all_to_all x2, starting transfers between devices, sum_at_owner(): pieces = lax.all_to_all(in_blocks(value, dim, size), axis, 0, 0, tiled=True)  16.3 us
    all_to_all x2, starting transfers between devices, copy_for_each(): return lax.all_to_all(copies, axis, split_axis=0, concat_axis=0, tiled=True)  15.5 us
  transfers between devices with their start and end apart: 39, of which 10 were waited for; matrix products, arithmetic and copies ran while one was open for 7% of the time, Pallas kernels for 0%

profile of v1, /device:TPU:8, one launch (start us, length us, event | category | flops | bytes accessed | tf_op | source)
XLA Modules:
  0.0 367.5 jit_solution(8332392556207893232)
XLA Ops:
  9.6 9.1 %all-to-all-start = ((f32[16,256,4]{1,2,0:T(4,128)}), f32[16,256,4]{1,2,0:T(4,128)S(1)}, u32[]{:S(2)}, u32[]{:S(2)}) async-start(f32[16,256,4]{1,2,0:T(4,128)} %bitcast.7), calls=%async_computation | async-start | bytes 131072 | tf_op jit(solution)/shard_map/all_to_all | solution.py:41
  23.0 3.2 fusion.44
  31.2 2.3 fusion.10
  33.5 2.0 dynamic-slice_select_fusion.1
  36.3 11.7 %all-to-all-start.1 = ((f32[32,256,4]{1,2,0:T(4,128)}), f32[32,256,4]{1,2,0:T(4,128)S(1)}, u32[]{:S(2)}, u32[]{:S(2)}) async-start(f32[32,256,4]{1,2,0:T(4,128)} %broadcast_in_dim.130), calls=%async_computation.1 | async-start | bytes 262144 | tf_op jit(solution)/shard_map/all_to_all | solution.py:47
  48.4 10.3 %all-to-all-done.1 = f32[32,256,4]{1,2,0:T(4,128)S(1)} async-done(((f32[32,256,4]{1,2,0:T(4,128)}), f32[32,256,4]{1,2,0:T(4,128)S(1)}, u32[]{:S(2)}, u32[]{:S(2)}) %all-to-all-start.1) | async-done | bytes 131104 | tf_op jit(solution)/shard_map/all_to_all | solution.py:47
  58.7 4.6 %all-to-all-start.2 = ((bf16[1,4,32,896]{3,1,0,2:T(4,128)(2,1)}), bf16[1,4,32,896]{3,1,0,2:T(4,128)(2,1)}, u32[]{:S(2)}, u32[]{:S(2)}) async-start(bf16[1,4,32,896]{3,1,0,2:T(4,128)(2,1)} %bitcast.12), calls=%async_computation.2 | async-start | bytes 458752 | tf_op jit(solution)/shard_map/all_to_all | solution.py:117
  64.1 10.6 %all-to-all-done.2 = bf16[1,4,32,896]{3,1,0,2:T(4,128)(2,1)} async-done(((bf16[1,4,32,896]{3,1,0,2:T(4,128)(2,1)}), bf16[1,4,32,896]{3,1,0,2:T(4,128)(2,1)}, u32[]{:S(2)}, u32[]{:S(2)}) %all-to-all-start.2) | async-done | bytes 229408 | tf_op jit(solution)/shard_map/all_to_all | solution.py:117
  80.5 7.2 %all-to-all-start.3 = ((f32[16,256,4]{1,2,0:T(4,128)}), f32[16,256,4]{1,2,0:T(4,128)S(1)}, u32[]{:S(2)}, u32[]{:S(2)}) async-start(f32[16,256,4]{1,2,0:T(4,128)} %bitcast.23), calls=%async_computation.4 | async-start | bytes 131072 | tf_op jit(solution)/shard_map/all_to_all | solution.py:41
  89.1 5.1 %all-to-all-done.3 = f32[16,256,4]{1,2,0:T(4,128)S(1)} async-done(((f32[16,256,4]{1,2,0:T(4,128)}), f32[16,256,4]{1,2,0:T(4,128)S(1)}, u32[]{:S(2)}, u32[]{:S(2)}) %all-to-all-start.3) | async-done | bytes 65568 | tf_op jit(solution)/shard_map/all_to_all | solution.py:41
  94.9 3.9 %all-to-all-start.4 = ((f32[32,256,4]{1,2,0:T(4,128)}), f32[32,256,4]{1,2,0:T(4,128)S(1)}, u32[]{:S(2)}, u32[]{:S(2)}) async-start(f32[32,256,4]{1,2,0:T(4,128)} %broadcast_in_dim.136), calls=%async_computation.5 | async-start | bytes 262144 | tf_op jit(solution)/shard_map/all_to_all | solution.py:47
  99.2 10.7 %all-to-all-done.4 = f32[32,256,4]{1,2,0:T(4,128)S(1)} async-done(((f32[32,256,4]{1,2,0:T(4,128)}), f32[32,256,4]{1,2,0:T(4,128)S(1)}, u32[]{:S(2)}, u32[]{:S(2)}) %all-to-all-start.4) | async-done | bytes 131104 | tf_op jit(solution)/shard_map/all_to_all | solution.py:47
  110.0 3.9 %all-to-all-start.5 = ((bf16[1,4,32,896]{3,1,0,2:T(4,128)(2,1)}), bf16[1,4,32,896]{3,1,0,2:T(4,128)(2,1)S(1)}, u32[]{:S(2)}, u32[]{:S(2)}) async-start(bf16[1,4,32,896]{3,1,0,2:T(4,128)(2,1)} %bitcast.28), calls=%async_computation.6 | async-start | bytes 458752 | tf_op jit(solution)/shard_map/all_to_all | solution.py:117
  114.1 11.6 %all-to-all-done.5 = bf16[1,4,32,896]{3,1,0,2:T(4,128)(2,1)S(1)} async-done(((bf16[1,4,32,896]{3,1,0,2:T(4,128)(2,1)}), bf16[1,4,32,896]{3,1,0,2:T(4,128)(2,1)S(1)}, u32[]{:S(2)}, u32[]{:S(2)}) %all-to-all-start.5) | async-done | bytes 229408 | tf_op jit(solution)/shard_map/all_to_all | solution.py:117
  128.7 4.0 %reduce-scatter.3.cloned.1.call-done = f32[16,1792]{1,0:T(8,128)} async-done(((f32[256,1792]{1,0:T(8,128)}), f32[16,1792]{1,0:T(8,128)}) %reduce-scatter.3.cloned.1.call-update) | async-done | bytes 114704 | tf_op jit(solution)/shard_map/reduce_scatter | solution.py:138
  133.6 1.7 collective-permute-start.1
  135.3 61.0 %reduce-scatter.5.cloned.1.call-done = f32[16,1792]{1,0:T(8,128)} async-done(((f32[256,1792]{1,0:T(8,128)}), f32[16,1792]{1,0:T(8,128)}) %reduce-scatter.5.cloned.1.call-update) | async-done | bytes 114704 | tf_op jit(solution)/shard_map/reduce_scatter | solution.py:138
  199.0 2.2 collective-permute-start.3
  201.3 2.7 collective-permute-start.18
  204.0 3.0 collective-permute-start.5
  207.0 3.0 collective-permute-start.20
  210.0 2.9 collective-permute-start.7
  213.0 3.0 collective-permute-start.22
  216.0 2.9 collective-permute-start.9
  219.0 3.0 collective-permute-start.24
  222.0 2.9 collective-permute-start.11
  225.0 3.0 collective-permute-start.26
  228.0 2.9 collective-permute-start.13
  231.0 3.0 collective-permute-start.28
  235.5 2.9 collective-permute-done.14
  241.0 87.0 %all-reduce.5.cloned.1.call-done = (f32[256,512]{1,0:T(8,128)}, f32[256,512]{1,0:T(8,128)}) async-done(((f32[256,512]{1,0:T(8,128)}, f32[256,512]{1,0:T(8,128)}), (f32[256,512]{1,0:T(8,128)}, f32[256,512]{1,0:T(8,128)})) %all-reduce.5.cloned.1.call-update) | async-done | bytes 1048592 | tf_op jit(solution)/shard_map/psum | solution.py:56
  327.9 32.1 %all-reduce.6 = (bf16[256,512]{1,0:T(8,128)(2,1)S(1)}, bf16[256,512]{1,0:T(8,128)(2,1)S(1)}) all-reduce(f32[256,512]{1,0:T(8,128)} %get-tuple-element.17, f32[256,512]{1,0:T(8,128)} %get-tuple-element.18), channel_id=1, replica_groups=mesh['pool_0'=8,'pool_1'=4,'tp'=16] {'pool_1'}, use_global_device_ids=true, to_apply=%region_20.22 | all-reduce | flops 262144 | bytes 1572864 | tf_op jit(solution)/shard_map/psum | solution.py:56
  (164 shorter events, 30.4 us)
Async XLA Ops:
  9.6 26.0 %all-to-all-start = ((f32[16,256,4]{1,2,0:T(4,128)}), f32[16,256,4]{1,2,0:T(4,128)S(1)}, u32[]{:S(2)}, u32[]{:S(2)}) async-start(f32[16,256,4]{1,2,0:T(4,128)} %bitcast.7), calls=%async_computation | async-start | bytes 131072 | tf_op jit(solution)/shard_map/all_to_all | solution.py:41
  36.3 22.4 %all-to-all-start.1 = ((f32[32,256,4]{1,2,0:T(4,128)}), f32[32,256,4]{1,2,0:T(4,128)S(1)}, u32[]{:S(2)}, u32[]{:S(2)}) async-start(f32[32,256,4]{1,2,0:T(4,128)} %broadcast_in_dim.130), calls=%async_computation.1 | async-start | bytes 262144 | tf_op jit(solution)/shard_map/all_to_all | solution.py:47
  58.7 16.0 %all-to-all-start.2 = ((bf16[1,4,32,896]{3,1,0,2:T(4,128)(2,1)}), bf16[1,4,32,896]{3,1,0,2:T(4,128)(2,1)}, u32[]{:S(2)}, u32[]{:S(2)}) async-start(bf16[1,4,32,896]{3,1,0,2:T(4,128)(2,1)} %bitcast.12), calls=%async_computation.2 | async-start | bytes 458752 | tf_op jit(solution)/shard_map/all_to_all | solution.py:117
  63.3 69.3 %reduce-scatter.3.cloned.1.call-start = ((), (), s32[]{:S(2)}) async-start(), calls=%async_computation.8 | async-start | bytes 1949696 | tf_op jit(solution)/shard_map/reduce_scatter | solution.py:138
  80.5 13.8 %all-to-all-start.3 = ((f32[16,256,4]{1,2,0:T(4,128)}), f32[16,256,4]{1,2,0:T(4,128)S(1)}, u32[]{:S(2)}, u32[]{:S(2)}) async-start(f32[16,256,4]{1,2,0:T(4,128)} %bitcast.23), calls=%async_computation.4 | async-start | bytes 131072 | tf_op jit(solution)/shard_map/all_to_all | solution.py:41
  94.9 15.1 %all-to-all-start.4 = ((f32[32,256,4]{1,2,0:T(4,128)}), f32[32,256,4]{1,2,0:T(4,128)S(1)}, u32[]{:S(2)}, u32[]{:S(2)}) async-start(f32[32,256,4]{1,2,0:T(4,128)} %broadcast_in_dim.136), calls=%async_computation.5 | async-start | bytes 262144 | tf_op jit(solution)/shard_map/all_to_all | solution.py:47
  110.0 15.7 %all-to-all-start.5 = ((bf16[1,4,32,896]{3,1,0,2:T(4,128)(2,1)}), bf16[1,4,32,896]{3,1,0,2:T(4,128)(2,1)S(1)}, u32[]{:S(2)}, u32[]{:S(2)}) async-start(bf16[1,4,32,896]{3,1,0,2:T(4,128)(2,1)} %bitcast.28), calls=%async_computation.6 | async-start | bytes 458752 | tf_op jit(solution)/shard_map/all_to_all | solution.py:117
  113.9 82.4 %reduce-scatter.5.cloned.1.call-start = ((), (), s32[]{:S(2)}) async-start(), calls=%async_computation.9 | async-start | bytes 1949696 | tf_op jit(solution)/shard_map/reduce_scatter | solution.py:138
  128.6 199.3 %all-reduce.5.cloned.1.call-start = ((), (), s32[]{:S(2)}) async-start(), calls=%async_computation.10 | async-start | bytes 2097152 | tf_op jit(solution)/shard_map/psum | solution.py:56
  133.5 65.4 %collective-permute-start = (bf16[16,896]{1,0:T(8,128)(2,1)S(1)}, bf16[16,896]{1,0:T(8,128)(2,1)S(1)}, u32[]{:S(2)}, u32[]{:S(2)}) collective-permute-start(bf16[16,896]{1,0:T(8,128)(2,1)S(1)} %get-tuple-element.22), channel_id=1, source_target_pairs={{0,1},{1,2},{2,3},{3,4},{4,5},{5,6},{6,7},{7,8},{8,9},{9,10},{10,1... | collective-permute-start | bytes 86024 | tf_op jit(solution)/shard_map/ppermute | solution.py:22
  133.6 65.4 %collective-permute-start.1 = (bf16[16,896]{1,0:T(8,128)(2,1)S(1)}, bf16[16,896]{1,0:T(8,128)(2,1)S(1)}, u32[]{:S(2)}, u32[]{:S(2)}) collective-permute-start(bf16[16,896]{1,0:T(8,128)(2,1)S(1)} %get-tuple-element.22), channel_id=1, source_target_pairs={{0,15},{1,0},{2,1},{3,2},{4,3},{5,4},{6,5},{7,6},{8,7},{9,8},{10,9... | collective-permute-start | bytes 86024 | tf_op jit(solution)/shard_map/ppermute | solution.py:27
  199.0 5.0 %collective-permute-start.3 = (bf16[16,896]{1,0:T(8,128)(2,1)S(1)}, bf16[16,896]{1,0:T(8,128)(2,1)S(1)}, u32[]{:S(2)}, u32[]{:S(2)}) collective-permute-start(bf16[16,896]{1,0:T(8,128)(2,1)S(1)} %collective-permute-done.1), channel_id=1, source_target_pairs={{0,15},{1,0},{2,1},{3,2},{4,3},{5,4},{6,5},{7,6},{8,7},{9,8},{10,9... | collective-permute-start | bytes 86024 | tf_op jit(solution)/shard_map/ppermute | solution.py:27
  201.2 5.7 %collective-permute-start.17 = (bf16[16,896]{1,0:T(8,128)(2,1)S(1)}, bf16[16,896]{1,0:T(8,128)(2,1)S(1)}, u32[]{:S(2)}, u32[]{:S(2)}) collective-permute-start(bf16[16,896]{1,0:T(8,128)(2,1)S(1)} %collective-permute-done.15), channel_id=1, source_target_pairs={{0,1},{1,2},{2,3},{3,4},{4,5},{5,6},{6,7},{7,8},{8,9},{9,10},{10,1... | collective-permute-start | bytes 86024 | tf_op jit(solution)/shard_map/ppermute | solution.py:22
  201.3 5.7 %collective-permute-start.18 = (bf16[16,896]{1,0:T(8,128)(2,1)S(1)}, bf16[16,896]{1,0:T(8,128)(2,1)S(1)}, u32[]{:S(2)}, u32[]{:S(2)}) collective-permute-start(bf16[16,896]{1,0:T(8,128)(2,1)S(1)} %collective-permute-done.16), channel_id=1, source_target_pairs={{0,15},{1,0},{2,1},{3,2},{4,3},{5,4},{6,5},{7,6},{8,7},{9,8},{10,9... | collective-permute-start | bytes 86024 | tf_op jit(solution)/shard_map/ppermute | solution.py:27
  204.0 6.0 %collective-permute-start.4 = (bf16[16,896]{1,0:T(8,128)(2,1)S(1)}, bf16[16,896]{1,0:T(8,128)(2,1)S(1)}, u32[]{:S(2)}, u32[]{:S(2)}) collective-permute-start(bf16[16,896]{1,0:T(8,128)(2,1)S(1)} %collective-permute-done.2), channel_id=1, source_target_pairs={{0,1},{1,2},{2,3},{3,4},{4,5},{5,6},{6,7},{7,8},{8,9},{9,10},{10,1... | collective-permute-start | bytes 86024 | tf_op jit(solution)/shard_map/ppermute | solution.py:22
  204.0 6.0 %collective-permute-start.5 = (bf16[16,896]{1,0:T(8,128)(2,1)S(1)}, bf16[16,896]{1,0:T(8,128)(2,1)S(1)}, u32[]{:S(2)}, u32[]{:S(2)}) collective-permute-start(bf16[16,896]{1,0:T(8,128)(2,1)S(1)} %collective-permute-done.3), channel_id=1, source_target_pairs={{0,15},{1,0},{2,1},{3,2},{4,3},{5,4},{6,5},{7,6},{8,7},{9,8},{10,9... | collective-permute-start | bytes 86024 | tf_op jit(solution)/shard_map/ppermute | solution.py:27
  207.0 6.0 %collective-permute-start.19 = (bf16[16,896]{1,0:T(8,128)(2,1)S(1)}, bf16[16,896]{1,0:T(8,128)(2,1)S(1)}, u32[]{:S(2)}, u32[]{:S(2)}) collective-permute-start(bf16[16,896]{1,0:T(8,128)(2,1)S(1)} %collective-permute-done.17), channel_id=1, source_target_pairs={{0,1},{1,2},{2,3},{3,4},{4,5},{5,6},{6,7},{7,8},{8,9},{9,10},{10,1... | collective-permute-start | bytes 86024 | tf_op jit(solution)/shard_map/ppermute | solution.py:22
  207.0 6.0 %collective-permute-start.20 = (bf16[16,896]{1,0:T(8,128)(2,1)S(1)}, bf16[16,896]{1,0:T(8,128)(2,1)S(1)}, u32[]{:S(2)}, u32[]{:S(2)}) collective-permute-start(bf16[16,896]{1,0:T(8,128)(2,1)S(1)} %collective-permute-done.18), channel_id=1, source_target_pairs={{0,15},{1,0},{2,1},{3,2},{4,3},{5,4},{6,5},{7,6},{8,7},{9,8},{10,9... | collective-permute-start | bytes 86024 | tf_op jit(solution)/shard_map/ppermute | solution.py:27
  210.0 6.0 %collective-permute-start.6 = (bf16[16,896]{1,0:T(8,128)(2,1)S(1)}, bf16[16,896]{1,0:T(8,128)(2,1)S(1)}, u32[]{:S(2)}, u32[]{:S(2)}) collective-permute-start(bf16[16,896]{1,0:T(8,128)(2,1)S(1)} %collective-permute-done.4), channel_id=1, source_target_pairs={{0,1},{1,2},{2,3},{3,4},{4,5},{5,6},{6,7},{7,8},{8,9},{9,10},{10,1... | collective-permute-start | bytes 86024 | tf_op jit(solution)/shard_map/ppermute | solution.py:22
  210.0 6.0 %collective-permute-start.7 = (bf16[16,896]{1,0:T(8,128)(2,1)S(1)}, bf16[16,896]{1,0:T(8,128)(2,1)S(1)}, u32[]{:S(2)}, u32[]{:S(2)}) collective-permute-start(bf16[16,896]{1,0:T(8,128)(2,1)S(1)} %collective-permute-done.5), channel_id=1, source_target_pairs={{0,15},{1,0},{2,1},{3,2},{4,3},{5,4},{6,5},{7,6},{8,7},{9,8},{10,9... | collective-permute-start | bytes 86024 | tf_op jit(solution)/shard_map/ppermute | solution.py:27
  212.9 6.0 %collective-permute-start.21 = (bf16[16,896]{1,0:T(8,128)(2,1)S(1)}, bf16[16,896]{1,0:T(8,128)(2,1)S(1)}, u32[]{:S(2)}, u32[]{:S(2)}) collective-permute-start(bf16[16,896]{1,0:T(8,128)(2,1)S(1)} %collective-permute-done.19), channel_id=1, source_target_pairs={{0,1},{1,2},{2,3},{3,4},{4,5},{5,6},{6,7},{7,8},{8,9},{9,10},{10,1... | collective-permute-start | bytes 86024 | tf_op jit(solution)/shard_map/ppermute | solution.py:22
  213.0 6.0 %collective-permute-start.22 = (bf16[16,896]{1,0:T(8,128)(2,1)S(1)}, bf16[16,896]{1,0:T(8,128)(2,1)S(1)}, u32[]{:S(2)}, u32[]{:S(2)}) collective-permute-start(bf16[16,896]{1,0:T(8,128)(2,1)S(1)} %collective-permute-done.20), channel_id=1, source_target_pairs={{0,15},{1,0},{2,1},{3,2},{4,3},{5,4},{6,5},{7,6},{8,7},{9,8},{10,9... | collective-permute-start | bytes 86024 | tf_op jit(solution)/shard_map/ppermute | solution.py:27
  216.0 6.0 %collective-permute-start.8 = (bf16[16,896]{1,0:T(8,128)(2,1)S(1)}, bf16[16,896]{1,0:T(8,128)(2,1)S(1)}, u32[]{:S(2)}, u32[]{:S(2)}) collective-permute-start(bf16[16,896]{1,0:T(8,128)(2,1)S(1)} %collective-permute-done.6), channel_id=1, source_target_pairs={{0,1},{1,2},{2,3},{3,4},{4,5},{5,6},{6,7},{7,8},{8,9},{9,10},{10,1... | collective-permute-start | bytes 86024 | tf_op jit(solution)/shard_map/ppermute | solution.py:22
  216.0 6.0 %collective-permute-start.9 = (bf16[16,896]{1,0:T(8,128)(2,1)S(1)}, bf16[16,896]{1,0:T(8,128)(2,1)S(1)}, u32[]{:S(2)}, u32[]{:S(2)}) collective-permute-start(bf16[16,896]{1,0:T(8,128)(2,1)S(1)} %collective-permute-done.7), channel_id=1, source_target_pairs={{0,15},{1,0},{2,1},{3,2},{4,3},{5,4},{6,5},{7,6},{8,7},{9,8},{10,9... | collective-permute-start | bytes 86024 | tf_op jit(solution)/shard_map/ppermute | solution.py:27
  218.9 6.0 %collective-permute-start.23 = (bf16[16,896]{1,0:T(8,128)(2,1)S(1)}, bf16[16,896]{1,0:T(8,128)(2,1)S(1)}, u32[]{:S(2)}, u32[]{:S(2)}) collective-permute-start(bf16[16,896]{1,0:T(8,128)(2,1)S(1)} %collective-permute-done.21), channel_id=1, source_target_pairs={{0,1},{1,2},{2,3},{3,4},{4,5},{5,6},{6,7},{7,8},{8,9},{9,10},{10,1... | collective-permute-start | bytes 86024 | tf_op jit(solution)/shard_map/ppermute | solution.py:22
  219.0 6.0 %collective-permute-start.24 = (bf16[16,896]{1,0:T(8,128)(2,1)S(1)}, bf16[16,896]{1,0:T(8,128)(2,1)S(1)}, u32[]{:S(2)}, u32[]{:S(2)}) collective-permute-start(bf16[16,896]{1,0:T(8,128)(2,1)S(1)} %collective-permute-done.22), channel_id=1, source_target_pairs={{0,15},{1,0},{2,1},{3,2},{4,3},{5,4},{6,5},{7,6},{8,7},{9,8},{10,9... | collective-permute-start | bytes 86024 | tf_op jit(solution)/shard_map/ppermute | solution.py:27
  222.0 6.0 %collective-permute-start.10 = (bf16[16,896]{1,0:T(8,128)(2,1)S(1)}, bf16[16,896]{1,0:T(8,128)(2,1)S(1)}, u32[]{:S(2)}, u32[]{:S(2)}) collective-permute-start(bf16[16,896]{1,0:T(8,128)(2,1)S(1)} %collective-permute-done.8), channel_id=1, source_target_pairs={{0,1},{1,2},{2,3},{3,4},{4,5},{5,6},{6,7},{7,8},{8,9},{9,10},{10,1... | collective-permute-start | bytes 86024 | tf_op jit(solution)/shard_map/ppermute | solution.py:22
  222.0 6.0 %collective-permute-start.11 = (bf16[16,896]{1,0:T(8,128)(2,1)S(1)}, bf16[16,896]{1,0:T(8,128)(2,1)S(1)}, u32[]{:S(2)}, u32[]{:S(2)}) collective-permute-start(bf16[16,896]{1,0:T(8,128)(2,1)S(1)} %collective-permute-done.9), channel_id=1, source_target_pairs={{0,15},{1,0},{2,1},{3,2},{4,3},{5,4},{6,5},{7,6},{8,7},{9,8},{10,9... | collective-permute-start | bytes 86024 | tf_op jit(solution)/shard_map/ppermute | solution.py:27
  224.9 6.0 %collective-permute-start.25 = (bf16[16,896]{1,0:T(8,128)(2,1)S(1)}, bf16[16,896]{1,0:T(8,128)(2,1)S(1)}, u32[]{:S(2)}, u32[]{:S(2)}) collective-permute-start(bf16[16,896]{1,0:T(8,128)(2,1)S(1)} %collective-permute-done.23), channel_id=1, source_target_pairs={{0,1},{1,2},{2,3},{3,4},{4,5},{5,6},{6,7},{7,8},{8,9},{9,10},{10,1... | collective-permute-start | bytes 86024 | tf_op jit(solution)/shard_map/ppermute | solution.py:22
  225.0 6.0 %collective-permute-start.26 = (bf16[16,896]{1,0:T(8,128)(2,1)S(1)}, bf16[16,896]{1,0:T(8,128)(2,1)S(1)}, u32[]{:S(2)}, u32[]{:S(2)}) collective-permute-start(bf16[16,896]{1,0:T(8,128)(2,1)S(1)} %collective-permute-done.24), channel_id=1, source_target_pairs={{0,15},{1,0},{2,1},{3,2},{4,3},{5,4},{6,5},{7,6},{8,7},{9,8},{10,9... | collective-permute-start | bytes 86024 | tf_op jit(solution)/shard_map/ppermute | solution.py:27
  228.0 6.0 %collective-permute-start.12 = (bf16[16,896]{1,0:T(8,128)(2,1)S(1)}, bf16[16,896]{1,0:T(8,128)(2,1)S(1)}, u32[]{:S(2)}, u32[]{:S(2)}) collective-permute-start(bf16[16,896]{1,0:T(8,128)(2,1)S(1)} %collective-permute-done.10), channel_id=1, source_target_pairs={{0,1},{1,2},{2,3},{3,4},{4,5},{5,6},{6,7},{7,8},{8,9},{9,10},{10,1... | collective-permute-start | bytes 86024 | tf_op jit(solution)/shard_map/ppermute | solution.py:22
  228.0 7.5 %collective-permute-start.13 = (bf16[16,896]{1,0:T(8,128)(2,1)S(1)}, bf16[16,896]{1,0:T(8,128)(2,1)S(1)}, u32[]{:S(2)}, u32[]{:S(2)}) collective-permute-start(bf16[16,896]{1,0:T(8,128)(2,1)S(1)} %collective-permute-done.11), channel_id=1, source_target_pairs={{0,15},{1,0},{2,1},{3,2},{4,3},{5,4},{6,5},{7,6},{8,7},{9,8},{10,9... | collective-permute-start | bytes 86024 | tf_op jit(solution)/shard_map/ppermute | solution.py:27
  (12 other events, 207.3 us)
Sparse Core Ops, SparseCore 0:
  78.8 53.8 reduce-scatter.2
  135.4 60.7 reduce-scatter.4
  241.1 86.7 all-reduce.4
